TPU v7x, 32 devices: a whole 2x2x4 slice. The times are simulated.
32 devices in a mesh: case: 2 (over x), ax: 16 (over z, y, core).
Axes of the slice: x: 2, y: 2, z: 4, core: 2. Of those that a mesh axis runs over, the one named last changes fastest.
Arguments:
- populations: float32 [19, 32, 128, 128], P(None, 'ax', 'case'), parts along dimension 2, may hold values from 0 to 1, as said below
- solid_mask: int32 [32, 128, 128], P('ax', 'case'), parts along dimension 1, may hold values from 0 to 1, as said below
- link_flags: int32 [2, 32, 128, 128], P(None, 'ax', 'case'), parts along dimension 2, may hold values from 0 to 511, as said below
- inlet_cells: int32 [1024], P('case'), parts along dimension 0, may hold values from 0 to 8191, as said below
- pod_basis: float32 [512, 3, 512], P(None, None, 'ax'), may hold values from -0.15625 to 0.15625
- mri_frames: float32 [24, 6, 512], P(None, 'case', 'ax'), parts along dimension 1
- frame_index: int32 [1], replicated, may hold values from 0 to 23
Outputs:
- advanced_populations: float32 [19, 32, 128, 128], P(None, 'ax', 'case'), parts along dimension 2
- inflow: float32 [2, 6, 512], P(None, 'case', 'ax'), parts along dimension 1
There are 2 independent parts, one for each index of `case`. A program takes and returns all parts, laid end to end along the dimension named above; an argument that names none is the same for every part. Nothing has to cross between parts.
Inputs may be any that keep to these rules, and one draw needn't show every extreme that they name: `solid_mask`: 1 marks a wall cell, 0 a fluid cell; the two outermost rows and columns of every cross-section are wall cells. `link_flags`: at a fluid cell, bit (i - 1) mod 9 of word (i - 1) div 9 is set exactly when the cell at minus c_i is a wall cell, the grid being continued past its first and last plane by repeating those planes; zero at wall cells. `inlet_cells`: distinct cells of the first plane, all of them fluid cells. `populations`: every entry is positive.
All inputs are finite; a program needn't handle non-finite values.
Results may differ from a plain program's by a relative error of at most 0.00011.
Values sent between devices are 32-bit elements; how exact they have to be, the bound alone decides.
A program may use at most 64 MiB of HBM per device.

v0:
```python
import math
import jax
import jax.numpy as jnp
from jax import lax
from jax.sharding import PartitionSpec as P

STEPS = 2
lattice_c = (
    (0, 0, 0),
    (1, 0, 0),
    (-1, 0, 0),
    (0, 1, 0),
    (0, -1, 0),
    (0, 0, 1),
    (0, 0, -1),
    (1, 1, 0),
    (-1, -1, 0),
    (1, -1, 0),
    (-1, 1, 0),
    (1, 0, 1),
    (-1, 0, -1),
    (1, 0, -1),
    (-1, 0, 1),
    (0, 1, 1),
    (0, -1, -1),
    (0, 1, -1),
    (0, -1, 1),
)
lattice_w = (1.0 / 3.0,) + (1.0 / 18.0,) * 6 + (1.0 / 36.0,) * 12
opposite_of = (0, 2, 1, 4, 3, 6, 5, 8, 7, 10, 9, 12, 11, 14, 13, 16, 15, 18, 17)
pair_list = ((0, 0), (1, 1), (2, 2), (0, 1), (0, 2), (1, 2))
relax_base = 0.52
smagorinsky_sq = 0.04
inflow_scale = 0.05


def extended(array, sides, width):
    for axis, dim in sides:
        count, length = (lax.axis_size(axis), array.shape[dim])
        up = [(i, (i + 1) % count) for i in range(count - 1)]
        down = [(j, i) for i, j in up]
        last = lax.slice_in_dim(array, length - width, length, axis=dim)
        leading = lax.slice_in_dim(array, 0, width, axis=dim)
        before = lax.ppermute(last, axis, up)
        after = lax.ppermute(leading, axis, down)
        array = jnp.concatenate([before, array, after], axis=dim)
    return array


def moment_rows():
    listed = [[1.0] * 19]
    for axis_a in range(3):
        listed.append([float(vector[axis_a]) for vector in lattice_c])
    for pair_a, pair_b in pair_list:
        listed.append([float(vector[pair_a] * vector[pair_b]) for vector in lattice_c])
    return jnp.asarray(listed, dtype=jnp.float32)


def equilibrium(density, velocity):
    lattice = jnp.asarray(
        [[float(entry) for entry in vector] for vector in lattice_c], dtype=jnp.float32
    )
    weights = jnp.asarray(list(lattice_w), dtype=jnp.float32).reshape((19,) + (1,) * density.ndim)
    projected = jnp.einsum("iq,q...->i...", lattice, velocity, precision=lax.Precision.HIGHEST)
    speed_sq = jnp.sum(velocity * velocity, axis=0)
    return (
        weights
        * density[None]
        * (1.0 + 3.0 * projected + 4.5 * projected * projected - 1.5 * speed_sq[None])
    )


def collide(populations, solid_mask):
    moments = jnp.einsum(
        "mi,i...->m...", moment_rows(), populations, precision=lax.Precision.HIGHEST
    )
    density = moments[0]
    velocity = moments[1:4] / density[None]
    nonequil = populations - equilibrium(density, velocity)
    stress = jnp.einsum(
        "mi,i...->m...", moment_rows()[4:], nonequil, precision=lax.Precision.HIGHEST
    )
    magnitude = stress[0] * stress[0] + stress[1] * stress[1] + stress[2] * stress[2]
    magnitude = magnitude + 2.0 * (
        stress[3] * stress[3] + stress[4] * stress[4] + stress[5] * stress[5]
    )
    relax_time = 0.5 * (
        relax_base
        + jnp.sqrt(
            relax_base * relax_base
            + 18.0 * math.sqrt(2.0) * smagorinsky_sq * jnp.sqrt(magnitude) / density
        )
    )
    relaxed = populations - nonequil / relax_time[None]
    return jnp.where(solid_mask[None] == 1, populations, relaxed)


def stream(relaxed, ghost_low, ghost_high, link_flags, solid_mask):
    padded = jnp.concatenate([ghost_low[:, None], relaxed, ghost_high[:, None]], axis=1)
    planes_here = relaxed.shape[1]
    read = []
    for direction in range(19):
        step_x, step_y, step_z = lattice_c[direction]
        source = padded[direction, 1 - step_z : 1 - step_z + planes_here]
        source = jnp.roll(source, (step_y, step_x), axis=(1, 2))
        if direction > 0:
            word = link_flags[(direction - 1) // 9]
            linked = jnp.bitwise_and(jnp.right_shift(word, (direction - 1) % 9), 1)
            source = jnp.where(linked == 1, relaxed[opposite_of[direction]], source)
        read.append(jnp.where(solid_mask == 1, relaxed[direction], source))
    return jnp.stack(read)


def inlet_plane(speeds, inlet_cells, height, plane_width):
    inlet_speed = jnp.zeros((3, height * plane_width), jnp.float32).at[:, inlet_cells].set(speeds)
    inlet_speed = inlet_speed.reshape(3, height, plane_width)
    return equilibrium(jnp.ones((height, plane_width), jnp.float32), inlet_speed)


def neighbour_planes(relaxed):
    padded = extended(relaxed, (("ax", 1),), 1)
    ghost_low = padded[:, 0]
    ghost_high = padded[:, -1]
    return (ghost_low, ghost_high)


def body(populations, solid_mask, link_flags, inlet_cells, pod_basis, mri_frames, frame_index):
    frames_total = mri_frames.shape[0]
    frame_slot = lax.broadcasted_iota(jnp.int32, (STEPS, frames_total), 1)
    segment_slot = lax.broadcasted_iota(jnp.int32, (STEPS, frames_total), 0)
    selector = (frame_slot == (frame_index[0] + segment_slot) % frames_total).astype(jnp.float32)
    chosen = jnp.einsum("sf,fjc->sjc", selector, mri_frames, precision=lax.Precision.HIGHEST)
    partial_terms = jnp.einsum("kjc,sjc->sk", pod_basis, chosen, precision=lax.Precision.HIGHEST)
    coefficients = lax.psum(partial_terms, "ax")
    local_inflow = jnp.einsum(
        "kjc,sk->sjc", pod_basis, coefficients, precision=lax.Precision.HIGHEST
    )
    whole_inflow = lax.all_gather(local_inflow, "ax", axis=2, tiled=True)
    position = lax.axis_index("ax")
    axis_count = lax.axis_size("ax")
    height = populations.shape[2]
    plane_width = populations.shape[3]
    for segment_index in range(STEPS):
        relaxed = collide(populations, solid_mask)
        inlet_ghost = inlet_plane(
            inflow_scale * whole_inflow[segment_index], inlet_cells, height, plane_width
        )
        ghost_low, ghost_high = neighbour_planes(relaxed)
        ghost_low = jnp.where(position == 0, inlet_ghost, ghost_low)
        ghost_high = jnp.where(position == axis_count - 1, relaxed[:, -1], ghost_high)
        populations = stream(relaxed, ghost_low, ghost_high, link_flags, solid_mask)
    return (populations, local_inflow)


def solution(mesh):
    in_specs = (
        P(None, "ax", "case", None),
        P("ax", "case", None),
        P(None, "ax", "case", None),
        P("case"),
        P(None, None, "ax"),
        P(None, "case", "ax"),
        P(),
    )
    out_specs = (P(None, "ax", "case", None), P(None, "case", "ax"))
    return jax.shard_map(body, mesh=mesh, in_specs=in_specs, out_specs=out_specs, check_vma=False)
```

profile of v0, /device:TPU:1, one launch (start us, length us, event | category | flops | bytes accessed | tf_op | source)
XLA Modules:
  0.0 146.1 jit_solution(2449302820524212767)
XLA Ops:
  0.6 0.9 broadcast_compare_fusion
  1.6 3.0 %fusion.4 = f32[10,2,64,128]{3,0,2,1:T(8,128)S(1)} fusion(f32[10,19,1,1]{1,0,3,2:T(8,128)} %constant.81, f32[19,2,64,128]{3,2,1,0:T(8,128)} %param.19), kind=kOutput, calls=%fused_computation.12 | convolution fusion | flops 37355520 | bytes 1901304 | tf_op jit(solution)/shard_map/mi,i...->m.../dot_general | solution.py:74
  4.9 1.5 %fusion.149 = f32[19,2,64,128]{3,0,2,1:T(8,128)S(1)} fusion(f32[19,3,1,1]{0,1,3,2:T(4,128)S(1)} %copy-done.22, f32[10,2,64,128]{3,0,2,1:T(8,128)S(1)} %fusion.4, f32[2,64,128]{2,1,0:T(8,128)S(1)} %bitcast.600), kind=kOutput, calls=%fused_computation.338 | convolution fusion | flops 11255808 | bytes 1574912 | tf_op jit(solution)/shard_map/iq,q...->i.../dot_general | solution.py:64
  6.4 0.4 copy_multiply_fusion.2
  6.8 0.8 copy-done.3
  7.7 2.8 %copy_subtract_fusion = f32[19,2,64,128]{3,0,2,1:T(8,128)S(1)} fusion(f32[19,2,64,128]{3,2,1,0:T(8,128)S(1)} %copy-done.3, f32[19,2,64,128]{3,2,1,0:T(8,128)S(1)} %get-tuple-element.100, f32[19,2,64,128]{3,2,1,0:T(8,128)S(1)} %get-tuple-element.61, f32[19,2,64,128]{3,0,2,1:T(8,128)S(1)} %fusion.149, f32[19,2,64,128]{3,2,1,0:T(8,128)S(1)} %get-tuple-element.60, ...), kind=kLoop, calls=%fused_computation.11 | loop fusion | flops 1556480 | bytes 7536640 | tf_op jit(solution)/shard_map/sub | solution.py:79
  10.5 0.9 fusion.171
  11.5 0.3 fusion.170
  11.9 1.0 subtract_select_fusion
  13.1 0.9 copy-done.5
  14.1 2.1 %collective-permute-start.1 = (f32[19,1,64,128]{3,2,1,0:T(8,128)S(1)}, f32[19,1,64,128]{3,2,1,0:T(8,128)}, u32[]{:S(2)}, u32[]{:S(2)}) collective-permute-start(f32[19,1,64,128]{3,2,1,0:T(8,128)S(1)} %slice.827), channel_id=1, source_target_pairs={{1,0},{2,1},{3,2},{4,3},{5,4},{6,5},{7,6},{8,7},{9,8},{10,9},{11,1... | collective-permute-start | bytes 1867784 | tf_op jit(solution)/shard_map/ppermute | solution.py:45
  16.1 0.6 slice_bitcast_fusion.36
  18.0 31.4 %psum.7 = f32[2,512]{1,0:T(2,128)S(1)} all-reduce(f32[2,512]{1,0:T(2,128)S(1)} %convolution_bitcast_fusion), channel_id=1, replica_groups=mesh['case'=2,'ax'=16] {'ax'}, use_global_device_ids=true, to_apply=%region_1.2 | all-reduce | flops 1024 | bytes 8192 | tf_op jit(solution)/shard_map/psum | solution.py:134
  49.3 1.0 fusion.139
  50.4 0.5 compare_select_fusion
  50.9 0.8 copy.150
  51.7 23.9 %all_gather.3 = f32[2,3,512]{1,0,2:T(2,128)S(1)} all-gather(f32[2,3,32]{1,0,2:T(2,128)S(1)} %copy.150), channel_id=1, replica_groups=mesh['case'=2,'ax'=16] {'ax'}, dimensions={2}, use_global_device_ids=true | all-gather | bytes 13056 | tf_op jit(solution)/shard_map/all_gather | solution.py:138
  75.6 1.4 slice_multiply_fusion
  77.1 0.6 constant_dynamic-update-slice_fusion.17
  77.7 0.6 copy-done.9
  78.3 0.7 slice.815
  79.0 4.3 %scatter_custom_fusion = f32[3,8192]{0,1:T(8,128)} fusion(s32[512]{0:T(512)} %compare_select_fusion, f32[512,3]{1,0:T(8,128)} %bitcast.636, f32[]{:T(128)} %constant.31.clone.1), kind=kCustom, calls=%fused_computation.7 | custom fusion | bytes 98816 | tf_op jit(solution)/shard_map/scatter | solution.py:115
  83.4 3.4 %multiply_reduce_fusion.1 = f32[8192]{0:T(1024)S(1)} fusion(f32[3,8192]{0,1:T(8,128)} %scatter_custom_fusion), kind=kLoop, calls=%fused_computation.3 | loop fusion | flops 40960 | bytes 131072 | tf_op jit(solution)/shard_map/reduce_sum | solution.py:65
  86.7 0.6 constant_dynamic-update-slice_fusion.16
  87.4 0.6 constant_dynamic-update-slice_fusion.15
  88.0 0.6 multiply_bitcast_fusion.3
  88.6 4.3 %scatter_custom_fusion.1 = f32[3,8192]{0,1:T(8,128)} fusion(s32[512]{0:T(512)} %compare_select_fusion, f32[512,3]{1,0:T(8,128)} %bitcast.635, f32[]{:T(128)} %constant.31.clone.1), kind=kCustom, calls=%fused_computation.5 | custom fusion | bytes 98816 | tf_op jit(solution)/shard_map/scatter | solution.py:115
  92.9 3.5 %multiply_reduce_fusion = f32[8192]{0:T(1024)S(1)} fusion(f32[3,8192]{0,1:T(8,128)} %scatter_custom_fusion.1), kind=kLoop, calls=%fused_computation.2 | loop fusion | flops 40960 | bytes 131072 | tf_op jit(solution)/shard_map/reduce_sum | solution.py:65
  96.4 4.6 %fusion.172 = f32[19,64,128]{2,0,1:T(8,128)} fusion(f32[19,3,1]{0,1,2:T(4,128)S(1)} %copy-done.24, f32[3,64,128]{0,2,1:T(8,128)S(1)} %bitcast.598), kind=kOutput, calls=%fused_computation.343 | convolution fusion | flops 5603328 | bytes 721124 | tf_op jit(solution)/shard_map/iq,q...->i.../dot_general | solution.py:64
  101.0 2.0 %bitcast_select_fusion = (f32[19,1,64,128]{3,2,1,0:T(8,128)S(1)}, f32[19,1,64,128]{3,2,1,0:T(8,128)}) fusion(f32[19,1,64,128]{3,2,1,0:T(8,128)} %collective-permute-done.1, pred[]{:T(512)S(6)} %eq.197, f32[19,2,64,128]{3,2,1,0:T(8,128)S(1)} %copy.143), kind=kLoop, calls=%fused_computation.45 | loop fusion | flops 155648 | bytes 2490369 | tf_op jit(solution)/shard_map/jit(_where)/select_n | solution.py:150
  103.1 3.9 %collective-permute-start = (f32[19,1,64,128]{3,2,1,0:T(8,128)}, f32[19,1,64,128]{3,2,1,0:T(8,128)}, u32[]{:S(2)}, u32[]{:S(2)}) collective-permute-start(f32[19,1,64,128]{3,2,1,0:T(8,128)} %get-tuple-element.80), channel_id=1, source_target_pairs={{0,1},{1,2},{2,3},{3,4},{4,5},{5,6},{6,7},{7,8},{8,9},{9,10},{10,1... | collective-permute-start | bytes 1867784 | tf_op jit(solution)/shard_map/ppermute | solution.py:44
  107.0 1.7 %slice.867 = f32[1,2,64,128]{3,0,2,1:T(1,128)} slice(f32[19,2,64,128]{3,0,2,1:T(8,128)} %copy-done.5), slice={[18:19], [0:2], [0:64], [0:128]} | slice | bytes 131072 | tf_op jit(solution)/shard_map/slice | solution.py:109
  108.8 0.6 slice.822
  109.3 0.6 slice.821
  110.0 0.9 constant_dynamic-update-slice_fusion.14
  110.9 5.6 %fusion.173 = f32[19,64,128]{2,0,1:T(8,128)S(1)} fusion(f32[19,3,1]{0,1,2:T(4,128)} %constant.84, f32[3,64,128]{0,2,1:T(8,128)} %bitcast.597), kind=kOutput, calls=%fused_computation.344 | convolution fusion | flops 5603328 | bytes 721124 | tf_op jit(solution)/shard_map/iq,q...->i.../dot_general | solution.py:64
  116.5 1.3 fusion.19
  119.6 0.4 copy-done.7
  120.2 1.7 %fusion.8 = f32[10,2,64,128]{3,0,2,1:T(8,128)S(1)} fusion(f32[10,19,1,1]{1,0,3,2:T(8,128)S(1)} %copy-done.19, f32[19,2,64,128]{3,2,1,0:T(8,128)S(1)} %get-tuple-element.2), kind=kOutput, calls=%fused_computation.16 | convolution fusion | flops 37355520 | bytes 1901304 | tf_op jit(solution)/shard_map/mi,i...->m.../dot_general | solution.py:74
  122.2 1.5 %fusion.150 = f32[19,2,64,128]{3,0,2,1:T(8,128)S(1)} fusion(f32[19,3,1,1]{0,1,3,2:T(4,128)S(1)} %copy-done.23, f32[10,2,64,128]{3,0,2,1:T(8,128)S(1)} %fusion.8, f32[2,64,128]{2,1,0:T(8,128)S(1)} %bitcast.604), kind=kOutput, calls=%fused_computation.339 | convolution fusion | flops 11255808 | bytes 1574912 | tf_op jit(solution)/shard_map/iq,q...->i.../dot_general | solution.py:64
  123.7 0.4 fusion.14
  124.4 1.6 %fusion.6 = f32[6,2,64,128]{3,0,2,1:T(8,128)S(1)} fusion(f32[6,19,1,1]{1,0,3,2:T(8,128)S(1)} %copy-done.21, f32[19,2,64,128]{3,2,1,0:T(8,128)S(1)} %fusion.14), kind=kOutput, calls=%fused_computation.14 | convolution fusion | flops 22413312 | bytes 1638856 | tf_op jit(solution)/shard_map/mi,i...->m.../dot_general | solution.py:80
  126.0 0.3 fusion.169
  126.4 0.3 subtract_select_fusion.1
  126.8 2.3 %collective-permute-start.2 = (f32[19,1,64,128]{3,2,0,1:T(8,128)S(1)}, f32[19,1,64,128]{3,2,0,1:T(8,128)S(1)}, u32[]{:S(2)}, u32[]{:S(2)}) collective-permute-start(f32[19,1,64,128]{3,2,0,1:T(8,128)S(1)} %get-tuple-element.67), channel_id=1, source_target_pairs={{0,1},{1,2},{2,3},{3,4},{4,5},{5,6},{6,7},{7,8},{8,9},{9,10},{10,1... | collective-permute-start | bytes 1867784 | tf_op jit(solution)/shard_map/ppermute | solution.py:44
  129.6 2.1 %collective-permute-start.3 = (f32[19,1,64,128]{3,2,0,1:T(8,128)S(1)}, f32[19,1,64,128]{3,2,0,1:T(8,128)S(1)}, u32[]{:S(2)}, u32[]{:S(2)}) collective-permute-start(f32[19,1,64,128]{3,2,0,1:T(8,128)S(1)} %get-tuple-element.66), channel_id=1, source_target_pairs={{1,0},{2,1},{3,2},{4,3},{5,4},{6,5},{7,6},{8,7},{9,8},{10,9},{11,1... | collective-permute-start | bytes 1867784 | tf_op jit(solution)/shard_map/ppermute | solution.py:45
  131.7 11.2 %collective-permute-done.2 = f32[19,1,64,128]{3,2,0,1:T(8,128)S(1)} collective-permute-done((f32[19,1,64,128]{3,2,0,1:T(8,128)S(1)}, f32[19,1,64,128]{3,2,0,1:T(8,128)S(1)}, u32[]{:S(2)}, u32[]{:S(2)}) %collective-permute-start.2) | collective-permute-done | bytes 622624 | tf_op jit(solution)/shard_map/ppermute | solution.py:44
  145.1 1.0 copy-done.27
  (156 shorter events, 6.2 us)
Async XLA Ops:
  0.6 17.1 %copy-start = (f32[512,3,32]{0,2,1:T(8,128)S(1)}, f32[512,3,32]{0,2,1:T(8,128)}, u32[]{:S(2)}) copy-start(f32[512,3,32]{0,2,1:T(8,128)} %param.23) | copy-start | bytes 589828
  1.5 3.3 %copy-start.22 = (f32[19,3,1,1]{0,1,3,2:T(4,128)S(1)}, f32[19,3,1,1]{0,1,3,2:T(4,128)}, u32[]{:S(2)}) copy-start(f32[19,3,1,1]{0,1,3,2:T(4,128)} %constant.82) | copy-start | bytes 688
  4.8 1.5 %copy-start.25 = (f32[19]{0:T(128)S(1)}, f32[19]{0:T(128)}, u32[]{:S(2)}) copy-start(f32[19]{0:T(128)} %constant.24.clone) | copy-start | bytes 232
  6.4 1.3 copy-start.3
  7.7 2.8 %copy-start.20 = (f32[6,19,1,1]{1,0,3,2:T(8,128)S(1)}, f32[6,19,1,1]{1,0,3,2:T(8,128)}, u32[]{:S(2)}) copy-start(f32[6,19,1,1]{1,0,3,2:T(8,128)} %constant.83) | copy-start | bytes 1372
  12.8 1.2 copy-start.5
  14.0 3.5 %copy-start.29 = (f32[24,3,32]{2,0,1:T(8,128)S(1)}, f32[24,3,32]{2,0,1:T(8,128)}, u32[]{:S(2)}) copy-start(f32[24,3,32]{2,0,1:T(8,128)} %param.24) | copy-start | bytes 27652
  14.0 36.4 %copy-start.28 = (s32[512]{0:T(512)S(1)}, s32[512]{0:T(512)}, u32[]{:S(2)}) copy-start(s32[512]{0:T(512)} %param.22) | copy-start | bytes 6148
  14.1 87.0 %collective-permute-start.1 = (f32[19,1,64,128]{3,2,1,0:T(8,128)S(1)}, f32[19,1,64,128]{3,2,1,0:T(8,128)}, u32[]{:S(2)}, u32[]{:S(2)}) collective-permute-start(f32[19,1,64,128]{3,2,1,0:T(8,128)S(1)} %slice.827), channel_id=1, source_target_pairs={{1,0},{2,1},{3,2},{4,3},{5,4},{6,5},{7,6},{8,7},{9,8},{10,9},{11,1... | collective-permute-start | bytes 1867784 | tf_op jit(solution)/shard_map/ppermute | solution.py:45
  16.8 60.3 %copy-start.1 = (s32[2,64,128]{2,1,0:T(8,128)S(1)}, s32[2,64,128]{2,1,0:T(8,128)}, u32[]{:S(2)}) copy-start(s32[2,64,128]{2,1,0:T(8,128)} %param.20) | copy-start | bytes 196612
  16.8 60.3 %copy-start.4 = (s32[2,2,64,128]{3,2,1,0:T(8,128)S(1)}, s32[2,2,64,128]{3,2,1,0:T(8,128)}, u32[]{:S(2)}) copy-start(s32[2,2,64,128]{3,2,1,0:T(8,128)} %param.21) | copy-start | bytes 393220
  51.7 25.3 %copy-start.8 = (f32[2,64,128]{2,1,0:T(8,128)S(1)}, f32[2,64,128]{2,1,0:T(8,128)}, u32[]{:S(2)}) copy-start(f32[2,64,128]{2,1,0:T(8,128)} %get-tuple-element.84) | copy-start | bytes 196612
  77.7 0.6 copy-start.9
  77.7 1.3 copy-start.12
  83.3 3.4 %copy-start.10 = (f32[2,64,128]{2,1,0:T(8,128)S(1)}, f32[2,64,128]{2,1,0:T(8,128)}, u32[]{:S(2)}) copy-start(f32[2,64,128]{2,1,0:T(8,128)} %copy-done.9) | copy-start | bytes 196612
  83.3 3.4 %copy-start.14 = (f32[2,64,127]{2,1,0:T(8,128)S(1)}, f32[2,64,127]{2,1,0:T(8,128)}, u32[]{:S(2)}) copy-start(f32[2,64,127]{2,1,0:T(8,128)} %slice.815) | copy-start | bytes 195076
  83.3 4.0 %copy-start.13 = (f32[2,64,128]{2,1,0:T(8,128)S(1)}, f32[2,64,128]{2,1,0:T(8,128)}, u32[]{:S(2)}) copy-start(f32[2,64,128]{2,1,0:T(8,128)} %copy-done.12) | copy-start | bytes 196612
  92.9 3.5 %copy-start.2 = (f32[3,8192]{0,1:T(8,128)S(1)}, f32[3,8192]{0,1:T(8,128)}, u32[]{:S(2)}) copy-start(f32[3,8192]{0,1:T(8,128)} %scatter_custom_fusion) | copy-start | bytes 294916
  92.9 3.5 %copy-start.24 = (f32[19,3,1]{0,1,2:T(4,128)S(1)}, f32[19,3,1]{0,1,2:T(4,128)}, u32[]{:S(2)}) copy-start(f32[19,3,1]{0,1,2:T(4,128)} %constant.84) | copy-start | bytes 688
  101.0 7.7 %copy-start.11 = (f32[2,64,128]{2,1,0:T(8,128)S(1)}, f32[2,64,128]{2,1,0:T(8,128)}, u32[]{:S(2)}) copy-start(f32[2,64,128]{2,1,0:T(8,128)} %get-tuple-element.81) | copy-start | bytes 196612
  103.1 13.4 %collective-permute-start = (f32[19,1,64,128]{3,2,1,0:T(8,128)}, f32[19,1,64,128]{3,2,1,0:T(8,128)}, u32[]{:S(2)}, u32[]{:S(2)}) collective-permute-start(f32[19,1,64,128]{3,2,1,0:T(8,128)} %get-tuple-element.80), channel_id=1, source_target_pairs={{0,1},{1,2},{2,3},{3,4},{4,5},{5,6},{6,7},{7,8},{8,9},{9,10},{10,1... | collective-permute-start | bytes 1867784 | tf_op jit(solution)/shard_map/ppermute | solution.py:44
  110.9 5.6 %copy-start.6 = (f32[19,64,128]{2,0,1:T(8,128)S(1)}, f32[19,64,128]{2,0,1:T(8,128)}, u32[]{:S(2)}) copy-start(f32[19,64,128]{2,0,1:T(8,128)} %fusion.172) | copy-start | bytes 1867780
  110.9 5.6 %copy-start.15 = (f32[64,128]{1,0:T(8,128)S(1)}, f32[64,128]{1,0:T(8,128)}, u32[]{:S(2)}) copy-start(f32[64,128]{1,0:T(8,128)} %multiply_bitcast_fusion.3) | copy-start | bytes 98308
  110.9 5.6 %copy-start.26 = (f32[19]{0:T(128)S(1)}, f32[19]{0:T(128)}, u32[]{:S(2)}) copy-start(f32[19]{0:T(128)} %constant.24.clone) | copy-start | bytes 232
  119.2 0.8 copy-start.7
  119.4 0.8 copy-start.19
  120.2 2.0 %copy-start.23 = (f32[19,3,1,1]{0,1,3,2:T(4,128)S(1)}, f32[19,3,1,1]{0,1,3,2:T(4,128)}, u32[]{:S(2)}) copy-start(f32[19,3,1,1]{0,1,3,2:T(4,128)} %constant.82) | copy-start | bytes 688
  123.7 0.7 copy-start.21
  126.7 2.5 %copy-start.16 = (pred[2,64,128]{2,1,0:T(8,128)(4,1)S(1)}, pred[2,64,128]{2,1,0:T(8,128)(4,1)}, u32[]{:S(2)}) copy-start(pred[2,64,128]{2,1,0:T(8,128)(4,1)} %get-tuple-element.37) | copy-start | bytes 49156
  126.7 2.7 %copy-start.18 = (pred[2,64,128]{2,1,0:T(8,128)(4,1)S(1)}, pred[2,64,128]{2,1,0:T(8,128)(4,1)}, u32[]{:S(2)}) copy-start(pred[2,64,128]{2,1,0:T(8,128)(4,1)} %get-tuple-element.35) | copy-start | bytes 49156
  126.8 2.7 %copy-start.17 = (pred[2,64,128]{2,1,0:T(8,128)(4,1)S(1)}, pred[2,64,128]{2,1,0:T(8,128)(4,1)}, u32[]{:S(2)}) copy-start(pred[2,64,128]{2,1,0:T(8,128)(4,1)} %get-tuple-element.33) | copy-start | bytes 49156
  126.8 16.1 %collective-permute-start.2 = (f32[19,1,64,128]{3,2,0,1:T(8,128)S(1)}, f32[19,1,64,128]{3,2,0,1:T(8,128)S(1)}, u32[]{:S(2)}, u32[]{:S(2)}) collective-permute-start(f32[19,1,64,128]{3,2,0,1:T(8,128)S(1)} %get-tuple-element.67), channel_id=1, source_target_pairs={{0,1},{1,2},{2,3},{3,4},{4,5},{5,6},{6,7},{7,8},{8,9},{9,10},{10,1... | collective-permute-start | bytes 1867784 | tf_op jit(solution)/shard_map/ppermute | solution.py:44
  129.6 13.7 %collective-permute-start.3 = (f32[19,1,64,128]{3,2,0,1:T(8,128)S(1)}, f32[19,1,64,128]{3,2,0,1:T(8,128)S(1)}, u32[]{:S(2)}, u32[]{:S(2)}) collective-permute-start(f32[19,1,64,128]{3,2,0,1:T(8,128)S(1)} %get-tuple-element.66), channel_id=1, source_target_pairs={{1,0},{2,1},{3,2},{4,3},{5,4},{6,5},{7,6},{8,7},{9,8},{10,9},{11,1... | collective-permute-start | bytes 1867784 | tf_op jit(solution)/shard_map/ppermute | solution.py:45
  145.1 1.0 copy-start.27
where the time goes:
time: 147 us; the launch traced here: 146 us
  blocking collectives  55.3 us (38%)
  other arithmetic  25.1 us (17%)
  matrix products  21.8 us (15%)
  local copies, waits for them, and re-layouts  20 us (14%)
  waiting for transfers between devices  11.2 us (8%)
  starting transfers between devices  10.4 us (7%)
  between operations  2.29 us (2%)
    psum x1, blocking collectives, body(): coefficients = lax.psum(partial_terms, 'ax')  31.4 us
    all_gather x1, blocking collectives, body(): whole_inflow = lax.all_gather(local_inflow, 'ax', axis=2, tiled=True)  23.9 us
    dot_general x4, matrix products, equilibrium(): jnp.einsum('iq,q...->i...', lattice, velocity, precision=lax.Precision.HI...  13.1 us
    ppermute x2, waiting for transfers between devices, extended(): before = lax.ppermute(last, axis, up)  11.2 us
    scatter x2, local copies, waits for them, and re-layouts, inlet_plane(): jnp.zeros((3, height * plane_width), jnp.float32).at[:, inlet_cells]  8.61 us
    reduce_sum x4, other arithmetic, equilibrium(): speed_sq = jnp.sum(velocity * velocity, axis=0)  7.34 us
    ppermute x2, starting transfers between devices, extended(): before = lax.ppermute(last, axis, up)  6.2 us
    dot_general x2, matrix products, collide(): jnp.einsum('mi,i...->m...', moment_rows(), populations, precision=lax.Pre...  4.7 us
  transfers between devices with their start and end apart: 4, of which 1 were waited for; matrix products, arithmetic and copies ran while one was open for 26% of the time, Pallas kernels for 0%

commit v1 on v0

--- a/solution.py
+++ b/solution.py
@@ -1,3 +1,4 @@
+import functools
 import math
 import jax
 import jax.numpy as jnp
@@ -32,6 +33,26 @@
 relax_base = 0.52
 smagorinsky_sq = 0.04
 inflow_scale = 0.05
+
+
+def _convert_ends(row_data, comm_axis):
+    nd = jax.lax.psum(1, comm_axis)
+    shelf = [(to_i, (to_i + 1) % nd) for to_i in range(nd)]
+    buffer = [(to_i, (to_i - 1) % nd) for to_i in range(nd)]
+    base_arr, t1 = ([row_data], [row_data])
+    for _ in range(nd // 2):
+        kept_arr = jax.lax.ppermute(base_arr[-1], comm_axis, shelf)
+        base_arr.append(kept_arr)
+    for _ in range((nd - 1) // 2):
+        block_now = jax.lax.ppermute(t1[-1], comm_axis, buffer)
+        t1.append(block_now)
+    formed = jnp.concatenate([*base_arr[::-1], *t1[1:]], 2)
+    vec_out = jax.lax.axis_index(comm_axis)
+    part_now = jnp.roll(formed, (vec_out - nd // 2) * row_data.shape[2], axis=2)
+    return part_now
+
+
+_settle_samples = functools.partial(_convert_ends, comm_axis="ax")
 
 
 def extended(array, sides, width):
@@ -135,7 +156,7 @@
     local_inflow = jnp.einsum(
         "kjc,sk->sjc", pod_basis, coefficients, precision=lax.Precision.HIGHEST
     )
-    whole_inflow = lax.all_gather(local_inflow, "ax", axis=2, tiled=True)
+    whole_inflow = _settle_samples(local_inflow)
     position = lax.axis_index("ax")
     axis_count = lax.axis_size("ax")
     height = populations.shape[2]

time: 147 us -> 156 us (1.061)
  starting transfers between devices: 10.4 us -> 41.4 us
  blocking collectives: 55.3 us -> 30.6 us
  waiting for transfers between devices: 11.2 us -> 20.8 us
  other arithmetic: 25.1 us -> 19.7 us
  matrix products: 21.8 us -> 19.3 us
    ppermute x0 -> x15, starting transfers between devices: none -> 26.7 us  [the longest x7 22.3 us: _convert_ends(): block_now = jax.lax.ppermute(t1[-1], comm_axis, buffer)]
    all_gather x1 -> x0, blocking collectives: 23.9 us -> none  [body(): whole_inflow = lax.all_gather(local_inflow, 'ax', axis=2, tiled=True)]
    ppermute x0 -> x15, waiting for transfers between devices: none -> 8.42 us  [the longest x8 4.38 us: _convert_ends(): kept_arr = jax.lax.ppermute(base_arr[-1], comm_axis, shelf)]
    ppermute x2, starting transfers between devices: 4.16 us -> 8.19 us  [extended(): after = lax.ppermute(leading, axis, down)]
    dot_general x4, matrix products: 13.1 us -> 10.4 us  [equilibrium(): jnp.einsum('iq,q...->i...', lattice, velocity, precision=lax.Precision.HI...]
    mul x0 -> x2, local copies, waits for them, and re-layouts: none -> 2.43 us  [body(): inflow_scale * whole_inflow[segment_index]]
    select_n x2, other arithmetic: 2.13 us -> 0.21 us  [body(): jnp.where(position == axis_count - 1, relaxed[:, -1], ghost_high)]
    slice x42, local copies, waits for them, and re-layouts: 2.95 us -> 1.14 us  [stream(): source = jnp.roll(source, (step_y, step_x), axis=(1, 2))]
  transfers between devices with their start and end apart: 4 -> 19, of which waited for: 1 -> 9; matrix products, arithmetic and copies ran while one was open for 26% -> 29% of each run, Pallas kernels for 0% -> 0%
where the time goes in v1:
time: 156 us; the launch traced here: 155 us
  starting transfers between devices  41.4 us (27%)
  blocking collectives  30.6 us (20%)
  local copies, waits for them, and re-layouts  21.1 us (14%)
  waiting for transfers between devices  20.8 us (13%)
  other arithmetic  19.7 us (13%)
  matrix products  19.3 us (12%)
  between operations  2.38 us (2%)
    psum x1, blocking collectives, body(): coefficients = lax.psum(partial_terms, 'ax')  30.6 us
    ppermute x7, starting transfers between devices, _convert_ends(): block_now = jax.lax.ppermute(t1[-1], comm_axis, buffer)  22.3 us
    ppermute x2, waiting for transfers between devices, extended(): before = lax.ppermute(last, axis, up)  11.7 us
    dot_general x4, matrix products, equilibrium(): jnp.einsum('iq,q...->i...', lattice, velocity, precision=lax.Precision.HI...  10.4 us
    scatter x2, local copies, waits for them, and re-layouts, inlet_plane(): jnp.zeros((3, height * plane_width), jnp.float32).at[:, inlet_cells]  8.63 us
    ppermute x2, starting transfers between devices, extended(): after = lax.ppermute(leading, axis, down)  8.19 us
    reduce_sum x4, other arithmetic, equilibrium(): speed_sq = jnp.sum(velocity * velocity, axis=0)  7.31 us
    ppermute x2, starting transfers between devices, extended(): before = lax.ppermute(last, axis, up)  6.53 us
  transfers between devices with their start and end apart: 19, of which 9 were waited for; matrix products, arithmetic and copies ran while one was open for 29% of the time, Pallas kernels for 0%

profile of v1, /device:TPU:1, one launch (start us, length us, event | category | flops | bytes accessed | tf_op | source)
XLA Modules:
  0.0 155.2 jit_solution(8058942273767640119)
XLA Ops:
  1.4 1.0 fusion.141
  2.6 30.6 %psum.7 = f32[2,512]{1,0:T(2,128)S(1)} all-reduce(f32[2,512]{1,0:T(2,128)S(1)} %convolution_bitcast_fusion), channel_id=1, replica_groups=mesh['case'=2,'ax'=16] {'ax'}, use_global_device_ids=true, to_apply=%region_1.2 | all-reduce | flops 1024 | bytes 8192 | tf_op jit(solution)/shard_map/psum | solution.py:155
  33.6 1.1 collective-permute-start
  34.7 3.4 %collective-permute-start.8 = (f32[2,3,32]{2,0,1:T(2,128)S(1)}, f32[2,3,32]{2,0,1:T(2,128)S(1)}, u32[]{:S(2)}, u32[]{:S(2)}) collective-permute-start(f32[2,3,32]{2,0,1:T(2,128)S(1)} %fusion.139), channel_id=1, source_target_pairs={{0,15},{1,0},{2,1},{3,2},{4,3},{5,4},{6,5},{7,6},{8,7},{9,8},{10,9... | collective-permute-start | bytes 2312 | tf_op jit(solution)/shard_map/ppermute | solution.py:47
  38.1 3.0 %fusion.4 = f32[10,2,64,128]{3,0,2,1:T(8,128)S(1)} fusion(f32[10,19,1,1]{1,0,3,2:T(8,128)} %constant.107, f32[19,2,64,128]{3,2,1,0:T(8,128)} %param.19), kind=kOutput, calls=%fused_computation.12 | convolution fusion | flops 37355520 | bytes 1901304 | tf_op jit(solution)/shard_map/mi,i...->m.../dot_general | solution.py:95
  41.4 1.5 fusion.149
  43.4 0.8 copy-done.4
  44.2 2.8 %copy_subtract_fusion = f32[19,2,64,128]{3,0,2,1:T(8,128)S(1)} fusion(f32[19,2,64,128]{3,2,1,0:T(8,128)S(1)} %copy-done.4, f32[19,2,64,128]{3,2,1,0:T(8,128)S(1)} %get-tuple-element.100, f32[19,2,64,128]{3,2,1,0:T(8,128)S(1)} %get-tuple-element.61, f32[19,2,64,128]{3,0,2,1:T(8,128)S(1)} %fusion.149, f32[19,2,64,128]{3,2,1,0:T(8,128)S(1)} %get-tuple-element.60, ...), kind=kLoop, calls=%fused_computation.11 | loop fusion | flops 1556480 | bytes 7536640 | tf_op jit(solution)/shard_map/sub | solution.py:100
  47.1 0.9 fusion.171
  48.5 1.0 subtract_select_fusion
  49.7 0.9 copy-done.6
  50.6 0.9 slice.826
  51.5 6.3 %collective-permute-start.16 = (f32[19,1,64,128]{3,2,1,0:T(8,128)}, f32[19,1,64,128]{3,2,1,0:T(8,128)S(1)}, u32[]{:S(2)}, u32[]{:S(2)}) collective-permute-start(f32[19,1,64,128]{3,2,1,0:T(8,128)} %slice.826), channel_id=1, source_target_pairs={{1,0},{2,1},{3,2},{4,3},{5,4},{6,5},{7,6},{8,7},{9,8},{10,9},{11,1... | collective-permute-start | bytes 1867784 | tf_op jit(solution)/shard_map/ppermute | solution.py:66
  57.9 0.6 constant_dynamic-update-slice_fusion.17
  59.2 2.0 %collective-permute-start.2 = (f32[2,3,32]{2,0,1:T(2,128)S(1)}, f32[2,3,32]{2,0,1:T(2,128)S(1)}, u32[]{:S(2)}, u32[]{:S(2)}) collective-permute-start(f32[2,3,32]{2,0,1:T(2,128)S(1)} %collective-permute-done.1), channel_id=1, source_target_pairs={{0,1},{1,2},{2,3},{3,4},{4,5},{5,6},{6,7},{7,8},{8,9},{9,10},{10,1... | collective-permute-start | bytes 2312 | tf_op jit(solution)/shard_map/ppermute | solution.py:44
  61.3 0.6 constant_dynamic-update-slice_fusion.16
  61.9 1.4 collective-permute-done.9
  63.9 1.2 collective-permute-start.3
  65.0 0.6 constant_dynamic-update-slice_fusion.15
  65.7 0.6 collective-permute-done.10
  66.3 3.3 %collective-permute-start.11 = (f32[2,3,32]{2,0,1:T(2,128)S(1)}, f32[2,3,32]{2,0,1:T(2,128)}, u32[]{:S(2)}, u32[]{:S(2)}) collective-permute-start(f32[2,3,32]{2,0,1:T(2,128)S(1)} %collective-permute-done.10), channel_id=1, source_target_pairs={{0,15},{1,0},{2,1},{3,2},{4,3},{5,4},{6,5},{7,6},{8,7},{9,8},{10,9... | collective-permute-start | bytes 2312 | tf_op jit(solution)/shard_map/ppermute | solution.py:47
  69.6 0.6 constant_dynamic-update-slice_fusion.14
  70.5 4.8 %collective-permute-start.12 = (f32[2,3,32]{2,0,1:T(2,128)}, f32[2,3,32]{2,0,1:T(2,128)}, u32[]{:S(2)}, u32[]{:S(2)}) collective-permute-start(f32[2,3,32]{2,0,1:T(2,128)} %collective-permute-done.11), channel_id=1, source_target_pairs={{0,15},{1,0},{2,1},{3,2},{4,3},{5,4},{6,5},{7,6},{8,7},{9,8},{10,9... | collective-permute-start | bytes 2312 | tf_op jit(solution)/shard_map/ppermute | solution.py:47
  76.5 4.9 %collective-permute-start.13 = (f32[2,3,32]{2,0,1:T(2,128)}, f32[2,3,32]{2,0,1:T(2,128)}, u32[]{:S(2)}, u32[]{:S(2)}) collective-permute-start(f32[2,3,32]{2,0,1:T(2,128)} %collective-permute-done.12), channel_id=1, source_target_pairs={{0,15},{1,0},{2,1},{3,2},{4,3},{5,4},{6,5},{7,6},{8,7},{9,8},{10,9... | collective-permute-start | bytes 2312 | tf_op jit(solution)/shard_map/ppermute | solution.py:47
  81.4 1.1 collective-permute-done.13
  82.5 4.9 %collective-permute-start.14 = (f32[2,3,32]{2,0,1:T(2,128)}, f32[2,3,32]{2,0,1:T(2,128)}, u32[]{:S(2)}, u32[]{:S(2)}) collective-permute-start(f32[2,3,32]{2,0,1:T(2,128)} %collective-permute-done.13), channel_id=1, source_target_pairs={{0,15},{1,0},{2,1},{3,2},{4,3},{5,4},{6,5},{7,6},{8,7},{9,8},{10,9... | collective-permute-start | bytes 2312 | tf_op jit(solution)/shard_map/ppermute | solution.py:47
  87.4 1.7 %slice.866 = f32[1,2,64,128]{3,0,2,1:T(1,128)} slice(f32[19,2,64,128]{3,0,2,1:T(8,128)} %copy-done.6), slice={[18:19], [0:2], [0:64], [0:128]} | slice | bytes 131072 | tf_op jit(solution)/shard_map/slice | solution.py:130
  89.2 4.3 %collective-permute-done.7 = f32[2,3,32]{2,0,1:T(2,128)} collective-permute-done((f32[2,3,32]{2,0,1:T(2,128)}, f32[2,3,32]{2,0,1:T(2,128)}, u32[]{:S(2)}, u32[]{:S(2)}) %collective-permute-start.7) | collective-permute-done | bytes 800 | tf_op jit(solution)/shard_map/ppermute | solution.py:44
  93.5 1.0 concatenate.172
  94.5 0.7 dynamic-slice_multiply_fusion
  95.2 0.9 copy.98
  96.0 4.3 %scatter_custom_fusion = f32[3,8192]{0,1:T(8,128)} fusion(s32[512]{0:T(512)} %compare_select_fusion, f32[512,3]{1,0:T(8,128)} %copy.98, f32[]{:T(128)} %constant.36.clone.1), kind=kCustom, calls=%fused_computation.7 | custom fusion | bytes 98816 | tf_op jit(solution)/shard_map/scatter | solution.py:136
  100.4 3.3 %multiply_reduce_fusion.1 = f32[8192]{0:T(1024)S(1)} fusion(f32[3,8192]{0,1:T(8,128)} %scatter_custom_fusion), kind=kLoop, calls=%fused_computation.3 | loop fusion | flops 40960 | bytes 131072 | tf_op jit(solution)/shard_map/reduce_sum | solution.py:86
  104.3 1.6 %copy.132 = f32[512,3]{1,0:T(8,128)} copy(f32[512,3]{0,1:T(4,128)} %bitcast.650) | data formatting | bytes 12288 | tf_op jit(solution)/shard_map/mul | solution.py:167
  105.9 4.3 %scatter_custom_fusion.1 = f32[3,8192]{0,1:T(8,128)} fusion(s32[512]{0:T(512)} %compare_select_fusion, f32[512,3]{1,0:T(8,128)} %copy.132, f32[]{:T(128)} %constant.36.clone.1), kind=kCustom, calls=%fused_computation.5 | custom fusion | bytes 98816 | tf_op jit(solution)/shard_map/scatter | solution.py:136
  110.2 3.5 %multiply_reduce_fusion = f32[8192]{0:T(1024)S(1)} fusion(f32[3,8192]{0,1:T(8,128)} %scatter_custom_fusion.1), kind=kLoop, calls=%fused_computation.2 | loop fusion | flops 40960 | bytes 131072 | tf_op jit(solution)/shard_map/reduce_sum | solution.py:86
  113.7 3.7 %fusion.172 = f32[19,64,128]{2,0,1:T(8,128)S(1)} fusion(f32[19,3,1]{0,1,2:T(4,128)S(1)} %copy-done.25, f32[3,64,128]{0,2,1:T(8,128)S(1)} %bitcast.600), kind=kOutput, calls=%fused_computation.345 | convolution fusion | flops 5603328 | bytes 721124 | tf_op jit(solution)/shard_map/iq,q...->i.../dot_general | solution.py:85
  117.6 2.1 %collective-permute-start.15 = (f32[19,1,64,128]{3,2,1,0:T(8,128)S(1)}, f32[19,1,64,128]{3,2,1,0:T(8,128)S(1)}, u32[]{:S(2)}, u32[]{:S(2)}) collective-permute-start(f32[19,1,64,128]{3,2,1,0:T(8,128)S(1)} %get-tuple-element.80), channel_id=1, source_target_pairs={{0,1},{1,2},{2,3},{3,4},{4,5},{5,6},{6,7},{7,8},{8,9},{9,10},{10,1... | collective-permute-start | bytes 1867784 | tf_op jit(solution)/shard_map/ppermute | solution.py:65
  119.8 3.8 %fusion.173 = f32[19,64,128]{2,0,1:T(8,128)S(1)} fusion(f32[19,3,1]{0,1,2:T(4,128)S(1)} %copy-done.25, f32[3,64,128]{0,2,1:T(8,128)S(1)} %bitcast.599), kind=kOutput, calls=%fused_computation.346 | convolution fusion | flops 5603328 | bytes 721124 | tf_op jit(solution)/shard_map/iq,q...->i.../dot_general | solution.py:85
  123.6 3.1 %collective-permute-done.15 = f32[19,1,64,128]{3,2,1,0:T(8,128)S(1)} collective-permute-done((f32[19,1,64,128]{3,2,1,0:T(8,128)S(1)}, f32[19,1,64,128]{3,2,1,0:T(8,128)S(1)}, u32[]{:S(2)}, u32[]{:S(2)}) %collective-permute-start.15) | collective-permute-done | bytes 622624 | tf_op jit(solution)/shard_map/ppermute | solution.py:65
  129.3 1.7 %fusion.8 = f32[10,2,64,128]{3,0,2,1:T(8,128)S(1)} fusion(f32[10,19,1,1]{1,0,3,2:T(8,128)S(1)} %copy-done.12, f32[19,2,64,128]{3,2,1,0:T(8,128)S(1)} %get-tuple-element.2), kind=kOutput, calls=%fused_computation.16 | convolution fusion | flops 37355520 | bytes 1901304 | tf_op jit(solution)/shard_map/mi,i...->m.../dot_general | solution.py:95
  131.1 1.5 fusion.150
  133.5 1.6 %fusion.6 = f32[6,2,64,128]{3,0,2,1:T(8,128)S(1)} fusion(f32[6,19,1,1]{1,0,3,2:T(8,128)S(1)} %copy-done.16, f32[19,2,64,128]{3,2,1,0:T(8,128)S(1)} %fusion.14), kind=kOutput, calls=%fused_computation.14 | convolution fusion | flops 22413312 | bytes 1638856 | tf_op jit(solution)/shard_map/mi,i...->m.../dot_general | solution.py:101
  136.0 4.4 %collective-permute-start.17 = (f32[19,1,64,128]{3,2,0,1:T(8,128)S(1)}, f32[19,1,64,128]{3,2,0,1:T(8,128)S(1)}, u32[]{:S(2)}, u32[]{:S(2)}) collective-permute-start(f32[19,1,64,128]{3,2,0,1:T(8,128)S(1)} %get-tuple-element.67), channel_id=1, source_target_pairs={{0,1},{1,2},{2,3},{3,4},{4,5},{5,6},{6,7},{7,8},{8,9},{9,10},{10,1... | collective-permute-start | bytes 1867784 | tf_op jit(solution)/shard_map/ppermute | solution.py:65
  140.8 1.9 %collective-permute-start.18 = (f32[19,1,64,128]{3,2,0,1:T(8,128)S(1)}, f32[19,1,64,128]{3,2,0,1:T(8,128)S(1)}, u32[]{:S(2)}, u32[]{:S(2)}) collective-permute-start(f32[19,1,64,128]{3,2,0,1:T(8,128)S(1)} %get-tuple-element.66), channel_id=1, source_target_pairs={{1,0},{2,1},{3,2},{4,3},{5,4},{6,5},{7,6},{8,7},{9,8},{10,9},{11,1... | collective-permute-start | bytes 1867784 | tf_op jit(solution)/shard_map/ppermute | solution.py:66
  142.8 8.5 %collective-permute-done.17 = f32[19,1,64,128]{3,2,0,1:T(8,128)S(1)} collective-permute-done((f32[19,1,64,128]{3,2,0,1:T(8,128)S(1)}, f32[19,1,64,128]{3,2,0,1:T(8,128)S(1)}, u32[]{:S(2)}, u32[]{:S(2)}) %collective-permute-start.17) | collective-permute-done | bytes 622624 | tf_op jit(solution)/shard_map/ppermute | solution.py:65
  151.6 0.7 collective-permute-done.18
  154.2 1.0 copy-done.28
  (189 shorter events, 12.3 us)
Async XLA Ops:
  0.6 1.7 %copy-start = (f32[512,3,32]{0,2,1:T(8,128)S(1)}, f32[512,3,32]{0,2,1:T(8,128)}, u32[]{:S(2)}) copy-start(f32[512,3,32]{0,2,1:T(8,128)} %param.23) | copy-start | bytes 589828
  33.6 59.9 %copy-start.13 = (f32[2,3,32]{2,0,1:T(2,128)}, f32[2,3,32]{2,0,1:T(2,128)S(1)}, u32[]{:S(2)}) copy-start(f32[2,3,32]{2,0,1:T(2,128)S(1)} %fusion.139) | copy-start | bytes 2308
  33.6 7.8 %copy-start.23 = (f32[19,3,1,1]{0,1,3,2:T(4,128)S(1)}, f32[19,3,1,1]{0,1,3,2:T(4,128)}, u32[]{:S(2)}) copy-start(f32[19,3,1,1]{0,1,3,2:T(4,128)} %constant.108) | copy-start | bytes 688
  33.6 24.3 %collective-permute-start = (f32[2,3,32]{2,0,1:T(2,128)S(1)}, f32[2,3,32]{2,0,1:T(2,128)S(1)}, u32[]{:S(2)}, u32[]{:S(2)}) collective-permute-start(f32[2,3,32]{2,0,1:T(2,128)S(1)} %fusion.139), channel_id=1, source_target_pairs={{0,1},{1,2},{2,3},{3,4},{4,5},{5,6},{6,7},{7,8},{8,9},{9,10},{10,1... | collective-permute-start | bytes 2312 | tf_op jit(solution)/shard_map/ppermute | solution.py:44
  34.7 24.0 %collective-permute-start.8 = (f32[2,3,32]{2,0,1:T(2,128)S(1)}, f32[2,3,32]{2,0,1:T(2,128)S(1)}, u32[]{:S(2)}, u32[]{:S(2)}) collective-permute-start(f32[2,3,32]{2,0,1:T(2,128)S(1)} %fusion.139), channel_id=1, source_target_pairs={{0,15},{1,0},{2,1},{3,2},{4,3},{5,4},{6,5},{7,6},{8,7},{9,8},{10,9... | collective-permute-start | bytes 2312 | tf_op jit(solution)/shard_map/ppermute | solution.py:47
  41.4 1.5 copy-start.26
  42.9 1.3 copy-start.4
  44.2 2.8 %copy-start.15 = (f32[6,19,1,1]{1,0,3,2:T(8,128)S(1)}, f32[6,19,1,1]{1,0,3,2:T(8,128)}, u32[]{:S(2)}) copy-start(f32[6,19,1,1]{1,0,3,2:T(8,128)} %constant.109) | copy-start | bytes 1372
  47.1 1.3 copy-start.1
  49.4 1.2 copy-start.6
  50.6 7.3 %copy-start.5 = (s32[2,2,64,128]{3,2,1,0:T(8,128)S(1)}, s32[2,2,64,128]{3,2,1,0:T(8,128)}, u32[]{:S(2)}) copy-start(s32[2,2,64,128]{3,2,1,0:T(8,128)} %param.21) | copy-start | bytes 393220
  51.5 66.0 %collective-permute-start.16 = (f32[19,1,64,128]{3,2,1,0:T(8,128)}, f32[19,1,64,128]{3,2,1,0:T(8,128)S(1)}, u32[]{:S(2)}, u32[]{:S(2)}) collective-permute-start(f32[19,1,64,128]{3,2,1,0:T(8,128)} %slice.826), channel_id=1, source_target_pairs={{1,0},{2,1},{3,2},{4,3},{5,4},{6,5},{7,6},{8,7},{9,8},{10,9},{11,1... | collective-permute-start | bytes 1867784 | tf_op jit(solution)/shard_map/ppermute | solution.py:66
  57.8 17.6 %copy-start.29 = (s32[512]{0:T(512)S(1)}, s32[512]{0:T(512)}, u32[]{:S(2)}) copy-start(s32[512]{0:T(512)} %param.22) | copy-start | bytes 6148
  57.9 1.4 collective-permute-start.1
  58.7 30.5 %copy-start.17 = (f32[2,3,32]{2,0,1:T(2,128)}, f32[2,3,32]{2,0,1:T(2,128)S(1)}, u32[]{:S(2)}) copy-start(f32[2,3,32]{2,0,1:T(2,128)S(1)} %collective-permute-done.8) | copy-start | bytes 2308
  58.7 4.6 %collective-permute-start.9 = (f32[2,3,32]{2,0,1:T(2,128)S(1)}, f32[2,3,32]{2,0,1:T(2,128)S(1)}, u32[]{:S(2)}, u32[]{:S(2)}) collective-permute-start(f32[2,3,32]{2,0,1:T(2,128)S(1)} %collective-permute-done.8), channel_id=1, source_target_pairs={{0,15},{1,0},{2,1},{3,2},{4,3},{5,4},{6,5},{7,6},{8,7},{9,8},{10,9... | collective-permute-start | bytes 2312 | tf_op jit(solution)/shard_map/ppermute | solution.py:47
  59.2 29.9 %copy-start.18 = (f32[2,3,32]{2,0,1:T(2,128)}, f32[2,3,32]{2,0,1:T(2,128)S(1)}, u32[]{:S(2)}) copy-start(f32[2,3,32]{2,0,1:T(2,128)S(1)} %collective-permute-done.1) | copy-start | bytes 2308
  59.2 4.6 %collective-permute-start.2 = (f32[2,3,32]{2,0,1:T(2,128)S(1)}, f32[2,3,32]{2,0,1:T(2,128)S(1)}, u32[]{:S(2)}, u32[]{:S(2)}) collective-permute-start(f32[2,3,32]{2,0,1:T(2,128)S(1)} %collective-permute-done.1), channel_id=1, source_target_pairs={{0,1},{1,2},{2,3},{3,4},{4,5},{5,6},{6,7},{7,8},{8,9},{9,10},{10,1... | collective-permute-start | bytes 2312 | tf_op jit(solution)/shard_map/ppermute | solution.py:44
  63.3 25.9 %copy-start.19 = (f32[2,3,32]{2,0,1:T(2,128)}, f32[2,3,32]{2,0,1:T(2,128)S(1)}, u32[]{:S(2)}) copy-start(f32[2,3,32]{2,0,1:T(2,128)S(1)} %collective-permute-done.9) | copy-start | bytes 2308
  63.3 3.0 %collective-permute-start.10 = (f32[2,3,32]{2,0,1:T(2,128)S(1)}, f32[2,3,32]{2,0,1:T(2,128)S(1)}, u32[]{:S(2)}, u32[]{:S(2)}) collective-permute-start(f32[2,3,32]{2,0,1:T(2,128)S(1)} %collective-permute-done.9), channel_id=1, source_target_pairs={{0,15},{1,0},{2,1},{3,2},{4,3},{5,4},{6,5},{7,6},{8,7},{9,8},{10,9... | collective-permute-start | bytes 2312 | tf_op jit(solution)/shard_map/ppermute | solution.py:47
  63.9 25.3 %copy-start.20 = (f32[2,3,32]{2,0,1:T(2,128)}, f32[2,3,32]{2,0,1:T(2,128)S(1)}, u32[]{:S(2)}) copy-start(f32[2,3,32]{2,0,1:T(2,128)S(1)} %collective-permute-done.2) | copy-start | bytes 2308
  63.9 5.7 %collective-permute-start.3 = (f32[2,3,32]{2,0,1:T(2,128)S(1)}, f32[2,3,32]{2,0,1:T(2,128)S(1)}, u32[]{:S(2)}, u32[]{:S(2)}) collective-permute-start(f32[2,3,32]{2,0,1:T(2,128)S(1)} %collective-permute-done.2), channel_id=1, source_target_pairs={{0,1},{1,2},{2,3},{3,4},{4,5},{5,6},{6,7},{7,8},{8,9},{9,10},{10,1... | collective-permute-start | bytes 2312 | tf_op jit(solution)/shard_map/ppermute | solution.py:44
  66.3 22.9 %copy-start.21 = (f32[2,3,32]{2,0,1:T(2,128)}, f32[2,3,32]{2,0,1:T(2,128)S(1)}, u32[]{:S(2)}) copy-start(f32[2,3,32]{2,0,1:T(2,128)S(1)} %collective-permute-done.10) | copy-start | bytes 2308
  66.3 4.2 %collective-permute-start.11 = (f32[2,3,32]{2,0,1:T(2,128)S(1)}, f32[2,3,32]{2,0,1:T(2,128)}, u32[]{:S(2)}, u32[]{:S(2)}) collective-permute-start(f32[2,3,32]{2,0,1:T(2,128)S(1)} %collective-permute-done.10), channel_id=1, source_target_pairs={{0,15},{1,0},{2,1},{3,2},{4,3},{5,4},{6,5},{7,6},{8,7},{9,8},{10,9... | collective-permute-start | bytes 2312 | tf_op jit(solution)/shard_map/ppermute | solution.py:47
  69.6 19.6 %copy-start.22 = (f32[2,3,32]{2,0,1:T(2,128)}, f32[2,3,32]{2,0,1:T(2,128)S(1)}, u32[]{:S(2)}) copy-start(f32[2,3,32]{2,0,1:T(2,128)S(1)} %collective-permute-done.3) | copy-start | bytes 2308
  69.6 5.8 %collective-permute-start.4 = (f32[2,3,32]{2,0,1:T(2,128)S(1)}, f32[2,3,32]{2,0,1:T(2,128)}, u32[]{:S(2)}, u32[]{:S(2)}) collective-permute-start(f32[2,3,32]{2,0,1:T(2,128)S(1)} %collective-permute-done.3), channel_id=1, source_target_pairs={{0,1},{1,2},{2,3},{3,4},{4,5},{5,6},{6,7},{7,8},{8,9},{9,10},{10,1... | collective-permute-start | bytes 2312 | tf_op jit(solution)/shard_map/ppermute | solution.py:44
  70.5 5.9 %collective-permute-start.12 = (f32[2,3,32]{2,0,1:T(2,128)}, f32[2,3,32]{2,0,1:T(2,128)}, u32[]{:S(2)}, u32[]{:S(2)}) collective-permute-start(f32[2,3,32]{2,0,1:T(2,128)} %collective-permute-done.11), channel_id=1, source_target_pairs={{0,15},{1,0},{2,1},{3,2},{4,3},{5,4},{6,5},{7,6},{8,7},{9,8},{10,9... | collective-permute-start | bytes 2312 | tf_op jit(solution)/shard_map/ppermute | solution.py:47
  75.4 6.0 %collective-permute-start.5 = (f32[2,3,32]{2,0,1:T(2,128)}, f32[2,3,32]{2,0,1:T(2,128)}, u32[]{:S(2)}, u32[]{:S(2)}) collective-permute-start(f32[2,3,32]{2,0,1:T(2,128)} %collective-permute-done.4), channel_id=1, source_target_pairs={{0,1},{1,2},{2,3},{3,4},{4,5},{5,6},{6,7},{7,8},{8,9},{9,10},{10,1... | collective-permute-start | bytes 2312 | tf_op jit(solution)/shard_map/ppermute | solution.py:44
  76.5 6.0 %collective-permute-start.13 = (f32[2,3,32]{2,0,1:T(2,128)}, f32[2,3,32]{2,0,1:T(2,128)}, u32[]{:S(2)}, u32[]{:S(2)}) collective-permute-start(f32[2,3,32]{2,0,1:T(2,128)} %collective-permute-done.12), channel_id=1, source_target_pairs={{0,15},{1,0},{2,1},{3,2},{4,3},{5,4},{6,5},{7,6},{8,7},{9,8},{10,9... | collective-permute-start | bytes 2312 | tf_op jit(solution)/shard_map/ppermute | solution.py:47
  81.4 6.0 %collective-permute-start.6 = (f32[2,3,32]{2,0,1:T(2,128)}, f32[2,3,32]{2,0,1:T(2,128)}, u32[]{:S(2)}, u32[]{:S(2)}) collective-permute-start(f32[2,3,32]{2,0,1:T(2,128)} %collective-permute-done.5), channel_id=1, source_target_pairs={{0,1},{1,2},{2,3},{3,4},{4,5},{5,6},{6,7},{7,8},{8,9},{9,10},{10,1... | collective-permute-start | bytes 2312 | tf_op jit(solution)/shard_map/ppermute | solution.py:44
  82.5 6.6 %collective-permute-start.14 = (f32[2,3,32]{2,0,1:T(2,128)}, f32[2,3,32]{2,0,1:T(2,128)}, u32[]{:S(2)}, u32[]{:S(2)}) collective-permute-start(f32[2,3,32]{2,0,1:T(2,128)} %collective-permute-done.13), channel_id=1, source_target_pairs={{0,15},{1,0},{2,1},{3,2},{4,3},{5,4},{6,5},{7,6},{8,7},{9,8},{10,9... | collective-permute-start | bytes 2312 | tf_op jit(solution)/shard_map/ppermute | solution.py:47
  87.4 6.0 %collective-permute-start.7 = (f32[2,3,32]{2,0,1:T(2,128)}, f32[2,3,32]{2,0,1:T(2,128)}, u32[]{:S(2)}, u32[]{:S(2)}) collective-permute-start(f32[2,3,32]{2,0,1:T(2,128)} %collective-permute-done.6), channel_id=1, source_target_pairs={{0,1},{1,2},{2,3},{3,4},{4,5},{5,6},{6,7},{7,8},{8,9},{9,10},{10,1... | collective-permute-start | bytes 2312 | tf_op jit(solution)/shard_map/ppermute | solution.py:44
  100.4 3.4 %copy-start.14 = (f32[1,3,512]{2,0,1:T(1,128)S(1)}, f32[1,3,512]{2,0,1:T(1,128)}, u32[]{:S(2)}) copy-start(f32[1,3,512]{2,0,1:T(1,128)} %get-tuple-element.98) | copy-start | bytes 18436
  110.2 3.5 %copy-start.3 = (f32[3,8192]{0,1:T(8,128)S(1)}, f32[3,8192]{0,1:T(8,128)}, u32[]{:S(2)}) copy-start(f32[3,8192]{0,1:T(8,128)} %scatter_custom_fusion) | copy-start | bytes 294916
  110.2 3.5 %copy-start.25 = (f32[19,3,1]{0,1,2:T(4,128)S(1)}, f32[19,3,1]{0,1,2:T(4,128)}, u32[]{:S(2)}) copy-start(f32[19,3,1]{0,1,2:T(4,128)} %constant.110) | copy-start | bytes 688
  113.7 6.1 %copy-start.2 = (f32[3,8192]{0,1:T(8,128)S(1)}, f32[3,8192]{0,1:T(8,128)}, u32[]{:S(2)}) copy-start(f32[3,8192]{0,1:T(8,128)} %scatter_custom_fusion.1) | copy-start | bytes 294916
  117.6 9.1 %collective-permute-start.15 = (f32[19,1,64,128]{3,2,1,0:T(8,128)S(1)}, f32[19,1,64,128]{3,2,1,0:T(8,128)S(1)}, u32[]{:S(2)}, u32[]{:S(2)}) collective-permute-start(f32[19,1,64,128]{3,2,1,0:T(8,128)S(1)} %get-tuple-element.80), channel_id=1, source_target_pairs={{0,1},{1,2},{2,3},{3,4},{4,5},{5,6},{6,7},{7,8},{8,9},{9,10},{10,1... | collective-permute-start | bytes 1867784 | tf_op jit(solution)/shard_map/ppermute | solution.py:65
  119.8 6.9 %copy-start.27 = (f32[19]{0:T(128)S(1)}, f32[19]{0:T(128)}, u32[]{:S(2)}) copy-start(f32[19]{0:T(128)} %constant.101.clone) | copy-start | bytes 232
  128.4 0.8 copy-start.7
  128.5 0.8 copy-start.12
  129.3 1.8 %copy-start.24 = (f32[19,3,1,1]{0,1,3,2:T(4,128)S(1)}, f32[19,3,1,1]{0,1,3,2:T(4,128)}, u32[]{:S(2)}) copy-start(f32[19,3,1,1]{0,1,3,2:T(4,128)} %constant.108) | copy-start | bytes 688
  135.8 4.6 %copy-start.9 = (pred[2,64,128]{2,1,0:T(8,128)(4,1)S(1)}, pred[2,64,128]{2,1,0:T(8,128)(4,1)}, u32[]{:S(2)}) copy-start(pred[2,64,128]{2,1,0:T(8,128)(4,1)} %get-tuple-element.37) | copy-start | bytes 49156
  135.8 4.8 %copy-start.10 = (pred[2,64,128]{2,1,0:T(8,128)(4,1)S(1)}, pred[2,64,128]{2,1,0:T(8,128)(4,1)}, u32[]{:S(2)}) copy-start(pred[2,64,128]{2,1,0:T(8,128)(4,1)} %get-tuple-element.35) | copy-start | bytes 49156
  135.9 4.8 %copy-start.11 = (pred[2,64,128]{2,1,0:T(8,128)(4,1)S(1)}, pred[2,64,128]{2,1,0:T(8,128)(4,1)}, u32[]{:S(2)}) copy-start(pred[2,64,128]{2,1,0:T(8,128)(4,1)} %get-tuple-element.33) | copy-start | bytes 49156
  135.9 6.8 %copy-start.8 = (pred[2,64,128]{2,1,0:T(8,128)(4,1)S(1)}, pred[2,64,128]{2,1,0:T(8,128)(4,1)}, u32[]{:S(2)}) copy-start(pred[2,64,128]{2,1,0:T(8,128)(4,1)} %get-tuple-element.31) | copy-start | bytes 49156
  136.0 15.3 %collective-permute-start.17 = (f32[19,1,64,128]{3,2,0,1:T(8,128)S(1)}, f32[19,1,64,128]{3,2,0,1:T(8,128)S(1)}, u32[]{:S(2)}, u32[]{:S(2)}) collective-permute-start(f32[19,1,64,128]{3,2,0,1:T(8,128)S(1)} %get-tuple-element.67), channel_id=1, source_target_pairs={{0,1},{1,2},{2,3},{3,4},{4,5},{5,6},{6,7},{7,8},{8,9},{9,10},{10,1... | collective-permute-start | bytes 1867784 | tf_op jit(solution)/shard_map/ppermute | solution.py:65
  140.8 11.6 %collective-permute-start.18 = (f32[19,1,64,128]{3,2,0,1:T(8,128)S(1)}, f32[19,1,64,128]{3,2,0,1:T(8,128)S(1)}, u32[]{:S(2)}, u32[]{:S(2)}) collective-permute-start(f32[19,1,64,128]{3,2,0,1:T(8,128)S(1)} %get-tuple-element.66), channel_id=1, source_target_pairs={{1,0},{2,1},{3,2},{4,3},{5,4},{6,5},{7,6},{8,7},{9,8},{10,9},{11,1... | collective-permute-start | bytes 1867784 | tf_op jit(solution)/shard_map/ppermute | solution.py:66
  154.2 1.0 copy-start.28
  (1 other events, 0.7 us)
